TPU v7x, 128 devices: a whole 4x4x4 slice. The times are simulated.
128 devices in a mesh: seq: 16 (over x_lo, y, core), tp: 8 (over z, x_hi).
Axes of the slice: x: 4 (x_hi: 2, x_lo: 2; x = x_hi * 2 + x_lo), y: 4, z: 4, core: 2. Of those that a mesh axis runs over, the one named last changes fastest.
Arguments:
- queries: bfloat16 [8192, 7168], P('seq', 'tp'), may hold values from -6 to 6
- new_kv: bfloat16 [2, 8192, 1024], P(None, 'seq', 'tp'), may hold values from -60 to 60, as said below
- cache_now: bfloat16 [2, 32768, 1024], P(None, 'seq', 'tp'), may hold values from -60 to 60, as said below
- cache_prev: bfloat16 [2, 2, 32768, 1024], P(None, None, 'seq', 'tp'), may hold values from -6 to 6
- out_weight: bfloat16 [7168, 7168], P('tp'), may hold values from -0.0625 to 0.0625
- residual: bfloat16 [8192, 7168], P(('seq', 'tp')), may hold values from -6 to 6
- cached_len: int32 [16], replicated, may hold values from 1 to 1536, as said below
- new_len: int32 [16], replicated, may hold values from 128 to 512, as said below
- page_table: int32 [16, 16], replicated, may hold values from -1 to 255, as said below
- dest_group: int32 [16], replicated, may hold values from 0 to 7, as said below
Outputs:
- mixed: bfloat16 [8192, 7168], P(('seq', 'tp'))
- decode_caches: bfloat16 [2, 2, 32768, 1024], P(None, None, 'seq', 'tp')
Inputs may be any that keep to these rules, and one draw needn't show every extreme that they name: `cached_len`: one request has exactly 1536 cached tokens and 512 new ones. Request r's new tokens are the first new_len[r] of its 512 rows. `page_table`: entry (r, j) is device * 16 + slot of the page holding positions j * 128 to j * 128 + 127 of request r for j below ceil((cached_len[r] + new_len[r]) / 128), else -1; no page is named twice; pages j of one request with equal j // 1 lie on one device, and different such runs of one request on different devices. `dest_group`: decode group g is the seq indices 2 g and 2 g + 1; every group is named by exactly two requests. `new_kv`: keys lie within -6 to 6. `cache_now`: keys lie within -6 to 6.
All inputs are finite; a program needn't handle non-finite values.
Results may differ from a plain program's by a relative error of at most 0.013.
Values may be sent and summed in bfloat16 or wider, within the bound.
A program may use at most 128 MiB of HBM per device.

v0:
```python
import functools
import math

import jax
import jax.numpy as jnp
from jax import lax
from jax.experimental import pallas as pl
from jax.experimental.pallas import tpu as pltpu
from jax.sharding import PartitionSpec as P

MESH = pl.DeviceIdType.MESH
BF = jnp.bfloat16
F32 = jnp.float32

N_SEQ = 16
PAGE = 128
HEADS = 7
HD = 128
FRESH = 512
CACHE_PAGES = 12
CACHE_ROWS = CACHE_PAGES * PAGE
KEYS = CACHE_ROWS + FRESH
WIDTH = 7168
GW = 512
GROUPS = WIDTH // GW
ZA = 4
XB = 3
NZ = 2 * ZA
NX = 2 * XB
CHUNK = 512
MASKED = -1e30
EXP_SCALE = math.log2(math.e) / math.sqrt(HD)
Z_STEP = (2, 1, 3, 0)


def rdma(src, dst, ssem, rsem, dev):
    return pltpu.make_async_remote_copy(
        src_ref=src, dst_ref=dst, send_sem=ssem, recv_sem=rsem, device_id=dev, device_id_type=MESH
    )


def kernel(
    tab, q_hbm, nkv_hbm, cnow_hbm, cprev_hbm, w_hbm, res_hbm,
    mixed_ref, dec_ref,
    q_v, nkv_v, cnow_v, cprev_v, w_v, res_v,
    snow, rnow, sprev, rprev, stage,
    kb, vb, qs, sbuf, att, part,
    xs, zfar, znear, xr, xfar, xnear, zxs, zxr,
    ld_sem, now_ss, now_rs, prev_ss, prev_rs, core_sem,
    zfar_ss, zfar_rs, znear_ss, znear_rs, xr_ss, xr_rs, xfar_ss, xfar_rs, xnear_ss, xnear_rs,
    zx_ss, zx_rs,
):
    s = lax.axis_index("seq")
    t = lax.axis_index("tp")
    core = s % 2
    z = t // 2
    hi = t % 2
    z_up = ((z + 1) % 4) * 2 + hi
    z_dn = ((z + 3) % 4) * 2 + hi
    up = (s, z_up)
    down = (s, z_dn)
    across = (s, z * 2 + 1 - hi)
    mate = (s + 1 - 2 * core, t)

    loads = [
        pltpu.make_async_copy(cnow_hbm, cnow_v, ld_sem.at[0]),
        pltpu.make_async_copy(cprev_hbm, cprev_v, ld_sem.at[1]),
        pltpu.make_async_copy(q_hbm, q_v, ld_sem.at[2]),
        pltpu.make_async_copy(nkv_hbm, nkv_v, ld_sem.at[3]),
        pltpu.make_async_copy(w_hbm, w_v, ld_sem.at[4]),
        pltpu.make_async_copy(res_hbm, res_v, ld_sem.at[5]),
    ]
    for copy in loads:
        copy.start()

    barrier = pltpu.get_barrier_semaphore()

    def greet(k, _):
        pl.semaphore_signal(barrier, inc=1, device_id=((s + k) % N_SEQ, t), device_id_type=MESH)
        return 0

    lax.fori_loop(1, N_SEQ, greet, 0)
    for dev in (up, down, across):
        pl.semaphore_signal(barrier, inc=1, device_id=dev, device_id_type=MESH)

    loads[0].wait()

    def pick_now(k, _):
        d = (s + k) % N_SEQ
        slot = tab[d]
        for kv in range(2):
            snow[d, kv] = cnow_v[kv, slot]
        return 0

    lax.fori_loop(1, N_SEQ, pick_now, 0)
    own_slot = tab[s]
    for kv in range(2):
        rnow[s, kv] = cnow_v[kv, own_slot]
    pl.semaphore_wait(barrier, N_SEQ - 1 + 3)

    def now_copy(src, d):
        return rdma(snow.at[d], rnow.at[src], now_ss.at[d], now_rs.at[src], (d, t))

    def send_now(k, _):
        now_copy(s, (s + k) % N_SEQ).start()
        return 0

    lax.fori_loop(1, N_SEQ, send_now, 0)

    loads[1].wait()

    def prev_copy(src, d):
        return rdma(sprev.at[d], rprev.at[src], prev_ss.at[d], prev_rs.at[src], (d, t))

    def send_prev(k, _):
        d = (s + k) % N_SEQ
        slot = tab[16 + d]
        for lk in range(4):
            sprev[d, lk] = cprev_v[lk, slot]
        prev_copy(s, d).start()
        return 0

    lax.fori_loop(1, N_SEQ, send_prev, 0)
    own_prev = tab[16 + s]
    for lk in range(4):
        rprev[s, lk] = cprev_v[lk, own_prev]

    cached = tab[64]
    fresh_count = tab[65]
    total = tab[66]
    loads[3].wait()
    loads[2].wait()
    qs[:, HD:] = jnp.ones((HEADS * PAGE, HD), BF)
    vb[:, HD:] = jnp.ones((KEYS, HD), BF)
    kb[CACHE_ROWS:, :HD] = nkv_v[0]
    vb[CACHE_ROWS:, :HD] = nkv_v[1]
    kb[CACHE_ROWS:, HD:] = jnp.zeros((FRESH, HD), BF)

    def wait_now(k, _):
        src = (s + k) % N_SEQ
        now_copy(src, src).wait_recv()
        return 0

    lax.fori_loop(1, N_SEQ, wait_now, 0)

    def place_now(j, _):
        src = tab[32 + j]
        row = pl.multiple_of(j * PAGE, PAGE)
        kb[pl.ds(row, PAGE), :HD] = rnow[src, 0]
        vb[pl.ds(row, PAGE), :HD] = rnow[src, 1]
        pos = row + lax.broadcasted_iota(jnp.int32, (PAGE, HD), 0)
        lane = lax.broadcasted_iota(jnp.int32, (PAGE, HD), 1)
        kb[pl.ds(row, PAGE), HD:] = jnp.where((lane == 0) & (pos >= cached), MASKED, 0.0).astype(BF)
        return 0

    lax.fori_loop(0, CACHE_PAGES, place_now, 0)
    loads[4].wait()
    loads[5].wait()

    def zfar_copy(side):
        half = part.at[0, ZA * side : ZA * (side + 1)]
        return rdma(half, zfar.at[side], zfar_ss.at[side], zfar_rs.at[side], (up, down)[side])

    def znear_copy(side, g):
        i = side * NZ + g
        return rdma(
            part.at[1 + side, g], znear.at[side, g], znear_ss.at[i], znear_rs.at[i], (up, down)[side]
        )

    def xr_copy(rel):
        rows = pl.ds(pl.multiple_of((1 - hi) * 64, 64), 64)
        return rdma(part.at[rel, NZ:GROUPS, rows], xr.at[rel], xr_ss.at[rel], xr_rs.at[rel], across)

    def block(rel, _):
        zb = (z + jnp.where(rel == 0, 2, jnp.where(rel == 1, 1, jnp.where(rel == 2, 3, 0)))) % 4
        row = pl.multiple_of(zb * PAGE, PAGE)
        for h in range(HEADS):
            qs[h * PAGE : (h + 1) * PAGE, :HD] = q_v[pl.ds(row, PAGE), h * HD : (h + 1) * HD]
        top = None
        for ch in range(KEYS // CHUNK):
            sc = lax.dot_general(
                qs[...], kb[ch * CHUNK : (ch + 1) * CHUNK, :], (((1,), (1,)), ((), ())),
                preferred_element_type=F32,
            )
            if ch == KEYS // CHUNK - 1:
                qpos = row + lax.broadcasted_iota(jnp.int32, (PAGE, CHUNK), 0)
                kpos = lax.broadcasted_iota(jnp.int32, (PAGE, CHUNK), 1)
                bias = jnp.where(kpos <= qpos, 0.0, MASKED)
                sc = (sc.reshape(HEADS, PAGE, CHUNK) + bias[None]).reshape(HEADS * PAGE, CHUNK)
            sbuf[:, ch * CHUNK : (ch + 1) * CHUNK] = sc
            for i in range(CHUNK // 128):
                piece = sc[:, i * 128 : (i + 1) * 128]
                top = piece if top is None else jnp.maximum(top, piece)
        peak = jnp.max(top, axis=1, keepdims=True)
        acc = None
        for ch in range(KEYS // CHUNK):
            wts = jnp.exp2((sbuf[:, ch * CHUNK : (ch + 1) * CHUNK] - peak) * EXP_SCALE).astype(BF)
            prod = jnp.dot(wts, vb[ch * CHUNK : (ch + 1) * CHUNK, :], preferred_element_type=F32)
            acc = prod if acc is None else acc + prod
        out = acc[:, :HD] / acc[:, HD:]
        live = row + lax.broadcasted_iota(jnp.int32, (PAGE, HD), 0) < fresh_count
        for h in range(HEADS):
            att[:, h * HD : (h + 1) * HD] = jnp.where(live, out[h * PAGE : (h + 1) * PAGE], 0.0).astype(BF)

        def project(g, _):
            cols = pl.ds(pl.multiple_of(g * GW, GW), GW)
            part[rel, g] = jnp.dot(att[...], w_v[:, cols], preferred_element_type=F32).astype(BF)
            return 0

        lax.fori_loop(0, GROUPS, project, 0)

        @pl.when(rel == 0)
        def _():
            zfar_copy(0).start()
            zfar_copy(1).start()

        @pl.when(rel == 1)
        def _():
            for g in range(ZA, NZ):
                znear_copy(0, g).start()

        @pl.when(rel == 2)
        def _():
            for g in range(ZA):
                znear_copy(1, g).start()

        xr_copy(rel).start()
        return 0

    lax.fori_loop(0, 4, block, 0)

    zfar_copy(0).wait_recv()
    for g in range(ZA):
        part[1, g] = (part[1, g].astype(F32) + zfar[0, g].astype(F32)).astype(BF)
        znear_copy(0, g).start()
    zfar_copy(1).wait_recv()
    for g in range(ZA):
        part[2, ZA + g] = (part[2, ZA + g].astype(F32) + zfar[1, g].astype(F32)).astype(BF)
        znear_copy(1, ZA + g).start()

    mine = pl.ds(pl.multiple_of(hi * 64, 64), 64)
    other = pl.ds(pl.multiple_of((1 - hi) * 64, 64), 64)

    def pair_sum(rel):
        xr_copy(rel).wait_recv()
        for g in range(NX):
            xs[rel, g] = (part[rel, NZ + g, mine, :].astype(F32) + xr[rel, g].astype(F32)).astype(BF)

    def xfar_copy(side):
        half = xs.at[0, XB * side : XB * (side + 1)]
        return rdma(half, xfar.at[side], xfar_ss.at[side], xfar_rs.at[side], (up, down)[side])

    def xnear_copy(side, half):
        i = side * 2 + half
        cols = pl.ds(half * XB, XB)
        return rdma(
            xs.at[1 + side, cols], xnear.at[side, cols], xnear_ss.at[i], xnear_rs.at[i], (up, down)[side]
        )

    pair_sum(0)
    xfar_copy(0).start()
    xfar_copy(1).start()
    pair_sum(1)
    xnear_copy(0, 1).start()
    pair_sum(2)
    xnear_copy(1, 0).start()

    def wait_prev(k, _):
        src = (s + k) % N_SEQ
        prev_copy(src, src).wait_recv()
        return 0

    lax.fori_loop(1, N_SEQ, wait_prev, 0)
    core_copy = rdma(stage, dec_ref.at[:, core], core_sem.at[0], core_sem.at[1], mate)

    def place_other(jj, _):
        page = (1 - core) * 8 + jj
        src = tab[48 + page]
        keep = page * PAGE + lax.broadcasted_iota(jnp.int32, (PAGE, HD), 0) < total
        for lk in range(4):
            stage[lk, jj] = jnp.where(keep, rprev[src, lk], jnp.zeros((), BF))
        return 0

    def place_own(jj, _):
        page = core * 8 + jj
        src = tab[48 + page]
        keep = page * PAGE + lax.broadcasted_iota(jnp.int32, (PAGE, HD), 0) < total
        for lk in range(4):
            dec_ref[lk, core, jj] = jnp.where(keep, rprev[src, lk], jnp.zeros((), BF))
        return 0

    lax.fori_loop(0, 8, place_other, 0)
    core_copy.start()
    lax.fori_loop(0, 8, place_own, 0)

    def zx_copy(g):
        return rdma(zxs.at[g], zxr.at[g], zx_ss.at[g], zx_rs.at[g], across)

    order = [g for pair in zip(range(ZA), range(ZA, NZ)) for g in pair]
    for g in order:
        znear_copy(0, g).wait_recv()
        znear_copy(1, g).wait_recv()
        zxs[g] = (
            part[3, g, other, :].astype(F32) + znear[0, g, other, :].astype(F32) + znear[1, g, other, :].astype(F32)
        ).astype(BF)
        zx_copy(g).start()

    xfar_copy(0).wait_recv()
    for g in range(XB):
        xs[1, g] = (xs[1, g].astype(F32) + xfar[0, g].astype(F32)).astype(BF)
    xnear_copy(0, 0).start()
    xfar_copy(1).wait_recv()
    for g in range(XB):
        xs[2, XB + g] = (xs[2, XB + g].astype(F32) + xfar[1, g].astype(F32)).astype(BF)
    xnear_copy(1, 1).start()
    xr_copy(3).wait_recv()

    for g in order:
        zx_copy(g).wait_recv()
        cols = slice(g * GW, (g + 1) * GW)
        mixed_ref[:, cols] = (
            res_v[:, cols].astype(F32)
            + part[3, g, mine, :].astype(F32)
            + znear[0, g, mine, :].astype(F32)
            + znear[1, g, mine, :].astype(F32)
            + zxr[g].astype(F32)
        ).astype(BF)
    for side in range(2):
        for half in range(2):
            xnear_copy(side, half).wait_recv()
    for g in range(NX):
        cols = slice((NZ + g) * GW, (NZ + g + 1) * GW)
        mixed_ref[:, cols] = (
            res_v[:, cols].astype(F32)
            + part[3, NZ + g, mine, :].astype(F32)
            + xr[3, g].astype(F32)
            + xnear[0, g].astype(F32)
            + xnear[1, g].astype(F32)
        ).astype(BF)

    def drain(k, _):
        d = (s + k) % N_SEQ
        now_copy(s, d).wait_send()
        prev_copy(s, d).wait_send()
        return 0

    lax.fori_loop(1, N_SEQ, drain, 0)
    for side in range(2):
        zfar_copy(side).wait_send()
        xfar_copy(side).wait_send()
        for g in range(NZ):
            znear_copy(side, g).wait_send()
        for half in range(2):
            xnear_copy(side, half).wait_send()
    for rel in range(4):
        xr_copy(rel).wait_send()
    for g in range(NZ):
        zx_copy(g).wait_send()
    core_copy.wait_send()
    rdma(stage, dec_ref.at[:, 1 - core], core_sem.at[0], core_sem.at[1], mate).wait_recv()


def tables(cached_len, new_len, page_table, dest_group):
    s = lax.axis_index("seq")
    ids = jnp.arange(16, dtype=jnp.int32)
    owner = jnp.where(page_table >= 0, page_table // 16, -1)
    slot = page_table % 16
    slot_now = jnp.sum(jnp.where(owner == s, slot, 0), axis=1)
    same = dest_group[None, :] == dest_group[:, None]
    rank = jnp.sum((same & (ids[None, :] < ids[:, None])).astype(jnp.int32), axis=1)
    dest = 2 * dest_group + rank
    slot_prev = jnp.sum(jnp.where(dest[:, None] == ids[None, :], slot_now[:, None], 0), axis=0)
    source = jnp.maximum(owner, 0)
    src_now = jnp.sum(jnp.where((ids == s)[:, None], source, 0), axis=0)
    src_prev = jnp.sum(jnp.where((dest == s)[:, None], source, 0), axis=0)
    cached = jnp.sum(jnp.where(ids == s, cached_len, 0))
    fresh = jnp.sum(jnp.where(ids == s, new_len, 0))
    total = jnp.sum(jnp.where(dest == s, cached_len + new_len, 0))
    tail = jnp.where(ids == 0, cached, jnp.where(ids == 1, fresh, jnp.where(ids == 2, total, 0)))
    return jnp.concatenate([slot_now, slot_prev, src_now, src_prev, tail]).astype(jnp.int32)


def body(
    queries, new_kv, cache_now, cache_prev, out_weight, residual, cached_len, new_len, page_table, dest_group
):
    tab = tables(cached_len, new_len, page_table, dest_group)
    any_spec = pl.BlockSpec(memory_space=pl.ANY)
    dma = pltpu.SemaphoreType.DMA
    vm = pltpu.VMEM
    mixed, decoded = pl.pallas_call(
        kernel,
        out_shape=(
            jax.ShapeDtypeStruct((64, WIDTH), BF),
            jax.ShapeDtypeStruct((4, 2, 8, PAGE, HD), BF),
        ),
        in_specs=[pl.BlockSpec(memory_space=pltpu.SMEM)] + [any_spec] * 6,
        out_specs=(pl.BlockSpec(memory_space=pltpu.VMEM), pl.BlockSpec(memory_space=pltpu.VMEM)),
        scratch_shapes=[
            vm((FRESH, HEADS * HD), BF),
            vm((2, FRESH, HD), BF),
            vm((2, 16, PAGE, HD), BF),
            vm((4, 16, PAGE, HD), BF),
            vm((HEADS * HD, WIDTH), BF),
            vm((64, WIDTH), BF),
            vm((16, 2, PAGE, HD), BF),
            vm((16, 2, PAGE, HD), BF),
            vm((16, 4, PAGE, HD), BF),
            vm((16, 4, PAGE, HD), BF),
            vm((4, 8, PAGE, HD), BF),
            vm((KEYS, 2 * HD), BF),
            vm((KEYS, 2 * HD), BF),
            vm((HEADS * PAGE, 2 * HD), BF),
            vm((HEADS * PAGE, KEYS), F32),
            vm((PAGE, HEADS * HD), BF),
            vm((4, GROUPS, PAGE, GW), BF),
            vm((3, NX, 64, GW), BF),
            vm((2, ZA, PAGE, GW), BF),
            vm((2, NZ, PAGE, GW), BF),
            vm((4, NX, 64, GW), BF),
            vm((2, XB, 64, GW), BF),
            vm((2, NX, 64, GW), BF),
            vm((NZ, 64, GW), BF),
            vm((NZ, 64, GW), BF),
            dma((6,)),
            dma((16,)), dma((16,)), dma((16,)), dma((16,)), dma((2,)),
            dma((2,)), dma((2,)), dma((2 * NZ,)), dma((2 * NZ,)), dma((4,)), dma((4,)),
            dma((2,)), dma((2,)), dma((4,)), dma((4,)), dma((NZ,)), dma((NZ,)),
        ],
        compiler_params=pltpu.CompilerParams(
            collective_id=0, has_side_effects=True, vmem_limit_bytes=66_000_000
        ),
        name="prefill",
    )(
        tab,
        queries,
        new_kv,
        cache_now.reshape(2, 16, PAGE, HD),
        cache_prev.reshape(4, 16, PAGE, HD),
        out_weight,
        residual,
    )
    return mixed, decoded.reshape(2, 2, 2048, HD)


def solution(mesh):
    placed = (
        P("seq", "tp"),
        P(None, "seq", "tp"),
        P(None, "seq", "tp"),
        P(None, None, "seq", "tp"),
        P("tp", None),
        P(("seq", "tp"), None),
        P(),
        P(),
        P(),
        P(),
    )
    return jax.shard_map(
        body,
        mesh=mesh,
        in_specs=placed,
        out_specs=(P(("seq", "tp"), None), P(None, None, "seq", "tp")),
        check_vma=False,
    )
```

profile of v0, /device:TPU:40, one launch (start us, length us, event | category | flops | bytes accessed | tf_op | source)
XLA Modules:
  0.0 110.6 jit_solution(6512688651991412161)
XLA Ops:
  0.6 0.9 convert_reduce_fusion
  1.6 1.4 %select_reduce_fusion.5 = (s32[]{:T(128)}, s32[]{:T(128)}, s32[]{:T(128)}, pred[16]{0:T(512)(128)(4,1)S(1)}, s32[16]{0:T(128)S(1)}) fusion(s32[16]{0:T(128)} %param.16, s32[]{:T(128)S(6)} %axis_index.15, s32[16]{0:T(128)} %param.17, s32[16]{0:T(128)S(1)} %convert_reduce_fusion, s32[16]{0:T(128)} %param.19), kind=kLoop, calls=%fused_computation.23 | loop fusion | flops 173 | bytes 352 | tf_op jit(solution)/shard_map/reduce_sum | solution.py:376
  3.0 0.9 select_reduce_fusion
  3.9 0.1 select_reduce_fusion.2
  4.0 2.0 %compare_select_fusion.2 = s32[16]{0:T(128)S(1)} fusion(s32[]{:T(128)} %get-tuple-element.10, s32[]{:T(128)} %get-tuple-element.11, s32[]{:T(128)} %get-tuple-element.9), kind=kLoop, calls=%fused_computation.20 | loop fusion | flops 96 | bytes 76 | tf_op jit(solution)/shard_map/jit(_where)/select_n | solution.py:379
  6.0 0.6 concatenate.3.tab
  6.6 98.8 %prefill.1 = (bf16[64,7168]{1,0:T(8,128)(2,1)}, bf16[4,2,8,128,128]{4,3,2,1,0:T(8,128)(2,1)}) custom-call(s32[80]{0:T(128)} %concatenate.3.tab, bf16[512,896]{1,0:T(8,128)(2,1)} %q_hbm.1, bf16[2,512,128]{2,1,0:T(8,128)(2,1)} %nkv_hbm.1, bf16[2,16,128,128]{3,2,1,0:T(8,128)(2,1)} %bitcast.5, bf16[4,16,128,128]{3,2,1,0:T(8,128)(2,1)} %bitcast.4, ...), custom_call_target="tpu_custom_call" | custom-call | tf_op jit(solution)/shard_map/prefill/pallas_call | solution.py:390
  105.4 2.2 %copy.14 = bf16[64,7168]{1,0:T(8,128)(2,1)} copy(bf16[64,7168]{1,0:T(8,128)(2,1)} %get-tuple-element.16) | data formatting | bytes 1835008
  107.6 3.0 %copy.15 = bf16[2,2,2048,128]{3,2,1,0:T(8,128)(2,1)} copy(bf16[2,2,2048,128]{3,2,1,0:T(8,128)(2,1)} %bitcast.3) | data formatting | bytes 4194304
  (1 shorter events, 0.0 us)
where the time goes:
time: 111 us
  Pallas kernels  98.8 us (89%)
  local copies, waits for them, and re-layouts  5.8 us (5%)
  other arithmetic  5.33 us (5%)
    pallas_call x1, Pallas kernels, body(): pl.pallas_call(kernel, out_shape=(jax.ShapeDtypeStruct((64, WIDTH), BF),...  98.8 us
    unnamed x2, local copies, waits for them, and re-layouts  5.21 us

commit v1 on v0

--- a/solution.py
+++ b/solution.py
@@ -23,8 +23,8 @@
 WIDTH = 7168
 GW = 512
 GROUPS = WIDTH // GW
-ZA = 4
-XB = 3
+ZA = 5
+XB = 2
 NZ = 2 * ZA
 NX = 2 * XB
 CHUNK = 512
@@ -40,7 +40,7 @@
 
 
 def kernel(
-    tab, q_hbm, nkv_hbm, cnow_hbm, cprev_hbm, w_hbm, res_hbm,
+    cached_len, new_len, pages, groups, q_hbm, nkv_hbm, cnow_hbm, cprev_hbm, w_hbm, res_hbm,
     mixed_ref, dec_ref,
     q_v, nkv_v, cnow_v, cprev_v, w_v, res_v,
     snow, rnow, sprev, rprev, stage,
@@ -70,8 +70,8 @@
         pltpu.make_async_copy(w_hbm, w_v, ld_sem.at[4]),
         pltpu.make_async_copy(res_hbm, res_v, ld_sem.at[5]),
     ]
-    for copy in loads:
-        copy.start()
+    loads[0].start()
+    loads[1].start()
 
     barrier = pltpu.get_barrier_semaphore()
 
@@ -83,17 +83,35 @@
     for dev in (up, down, across):
         pl.semaphore_signal(barrier, inc=1, device_id=dev, device_id_type=MESH)
 
+    def slot_of(r):
+        slot = 0
+        for j in range(16):
+            entry = pages[r, j]
+            slot = jnp.where((entry >> 4) == s, entry & 15, slot)
+        return slot
+
+    def request_at(d):
+        first = 15
+        last = 0
+        for r in range(16):
+            mine = groups[r] == d // 2
+            first = jnp.minimum(first, jnp.where(mine, r, 15))
+            last = jnp.maximum(last, jnp.where(mine, r, 0))
+        return jnp.where(d % 2 == 0, first, last)
+
     loads[0].wait()
+    for copy in loads[2:]:
+        copy.start()
 
     def pick_now(k, _):
         d = (s + k) % N_SEQ
-        slot = tab[d]
+        slot = slot_of(d)
         for kv in range(2):
             snow[d, kv] = cnow_v[kv, slot]
         return 0
 
     lax.fori_loop(1, N_SEQ, pick_now, 0)
-    own_slot = tab[s]
+    own_slot = slot_of(s)
     for kv in range(2):
         rnow[s, kv] = cnow_v[kv, own_slot]
     pl.semaphore_wait(barrier, N_SEQ - 1 + 3)
@@ -114,20 +132,21 @@
 
     def send_prev(k, _):
         d = (s + k) % N_SEQ
-        slot = tab[16 + d]
+        slot = slot_of(request_at(d))
         for lk in range(4):
             sprev[d, lk] = cprev_v[lk, slot]
         prev_copy(s, d).start()
         return 0
 
     lax.fori_loop(1, N_SEQ, send_prev, 0)
-    own_prev = tab[16 + s]
+    moved = request_at(s)
+    own_prev = slot_of(moved)
     for lk in range(4):
         rprev[s, lk] = cprev_v[lk, own_prev]
 
-    cached = tab[64]
-    fresh_count = tab[65]
-    total = tab[66]
+    cached = cached_len[s]
+    fresh_count = new_len[s]
+    total = cached_len[moved] + new_len[moved]
     loads[3].wait()
     loads[2].wait()
     qs[:, HD:] = jnp.ones((HEADS * PAGE, HD), BF)
@@ -144,7 +163,7 @@
     lax.fori_loop(1, N_SEQ, wait_now, 0)
 
     def place_now(j, _):
-        src = tab[32 + j]
+        src = jnp.maximum(pages[s, j] >> 4, 0)
         row = pl.multiple_of(j * PAGE, PAGE)
         kb[pl.ds(row, PAGE), :HD] = rnow[src, 0]
         vb[pl.ds(row, PAGE), :HD] = rnow[src, 1]
@@ -172,6 +191,17 @@
         return rdma(part.at[rel, NZ:GROUPS, rows], xr.at[rel], xr_ss.at[rel], xr_rs.at[rel], across)
 
     def block(rel, _):
+        @pl.when(rel == 3)
+        def _():
+            zfar_copy(0).wait_recv()
+            for g in range(ZA):
+                part[1, g] = (part[1, g].astype(F32) + zfar[0, g].astype(F32)).astype(BF)
+                znear_copy(0, g).start()
+            zfar_copy(1).wait_recv()
+            for g in range(ZA):
+                part[2, ZA + g] = (part[2, ZA + g].astype(F32) + zfar[1, g].astype(F32)).astype(BF)
+                znear_copy(1, ZA + g).start()
+
         zb = (z + jnp.where(rel == 0, 2, jnp.where(rel == 1, 1, jnp.where(rel == 2, 3, 0)))) % 4
         row = pl.multiple_of(zb * PAGE, PAGE)
         for h in range(HEADS):
@@ -229,15 +259,6 @@
 
     lax.fori_loop(0, 4, block, 0)
 
-    zfar_copy(0).wait_recv()
-    for g in range(ZA):
-        part[1, g] = (part[1, g].astype(F32) + zfar[0, g].astype(F32)).astype(BF)
-        znear_copy(0, g).start()
-    zfar_copy(1).wait_recv()
-    for g in range(ZA):
-        part[2, ZA + g] = (part[2, ZA + g].astype(F32) + zfar[1, g].astype(F32)).astype(BF)
-        znear_copy(1, ZA + g).start()
-
     mine = pl.ds(pl.multiple_of(hi * 64, 64), 64)
     other = pl.ds(pl.multiple_of((1 - hi) * 64, 64), 64)
 
@@ -275,7 +296,7 @@
 
     def place_other(jj, _):
         page = (1 - core) * 8 + jj
-        src = tab[48 + page]
+        src = jnp.maximum(pages[moved, page] >> 4, 0)
         keep = page * PAGE + lax.broadcasted_iota(jnp.int32, (PAGE, HD), 0) < total
         for lk in range(4):
             stage[lk, jj] = jnp.where(keep, rprev[src, lk], jnp.zeros((), BF))
@@ -283,7 +304,7 @@
 
     def place_own(jj, _):
         page = core * 8 + jj
-        src = tab[48 + page]
+        src = jnp.maximum(pages[moved, page] >> 4, 0)
         keep = page * PAGE + lax.broadcasted_iota(jnp.int32, (PAGE, HD), 0) < total
         for lk in range(4):
             dec_ref[lk, core, jj] = jnp.where(keep, rprev[src, lk], jnp.zeros((), BF))
@@ -360,30 +381,9 @@
     rdma(stage, dec_ref.at[:, 1 - core], core_sem.at[0], core_sem.at[1], mate).wait_recv()
 
 
-def tables(cached_len, new_len, page_table, dest_group):
-    s = lax.axis_index("seq")
-    ids = jnp.arange(16, dtype=jnp.int32)
-    owner = jnp.where(page_table >= 0, page_table // 16, -1)
-    slot = page_table % 16
-    slot_now = jnp.sum(jnp.where(owner == s, slot, 0), axis=1)
-    same = dest_group[None, :] == dest_group[:, None]
-    rank = jnp.sum((same & (ids[None, :] < ids[:, None])).astype(jnp.int32), axis=1)
-    dest = 2 * dest_group + rank
-    slot_prev = jnp.sum(jnp.where(dest[:, None] == ids[None, :], slot_now[:, None], 0), axis=0)
-    source = jnp.maximum(owner, 0)
-    src_now = jnp.sum(jnp.where((ids == s)[:, None], source, 0), axis=0)
-    src_prev = jnp.sum(jnp.where((dest == s)[:, None], source, 0), axis=0)
-    cached = jnp.sum(jnp.where(ids == s, cached_len, 0))
-    fresh = jnp.sum(jnp.where(ids == s, new_len, 0))
-    total = jnp.sum(jnp.where(dest == s, cached_len + new_len, 0))
-    tail = jnp.where(ids == 0, cached, jnp.where(ids == 1, fresh, jnp.where(ids == 2, total, 0)))
-    return jnp.concatenate([slot_now, slot_prev, src_now, src_prev, tail]).astype(jnp.int32)
-
-
 def body(
     queries, new_kv, cache_now, cache_prev, out_weight, residual, cached_len, new_len, page_table, dest_group
 ):
-    tab = tables(cached_len, new_len, page_table, dest_group)
     any_spec = pl.BlockSpec(memory_space=pl.ANY)
     dma = pltpu.SemaphoreType.DMA
     vm = pltpu.VMEM
@@ -393,7 +393,7 @@
             jax.ShapeDtypeStruct((64, WIDTH), BF),
             jax.ShapeDtypeStruct((4, 2, 8, PAGE, HD), BF),
         ),
-        in_specs=[pl.BlockSpec(memory_space=pltpu.SMEM)] + [any_spec] * 6,
+        in_specs=[pl.BlockSpec(memory_space=pltpu.SMEM)] * 4 + [any_spec] * 6,
         out_specs=(pl.BlockSpec(memory_space=pltpu.VMEM), pl.BlockSpec(memory_space=pltpu.VMEM)),
         scratch_shapes=[
             vm((FRESH, HEADS * HD), BF),
@@ -431,7 +431,10 @@
         ),
         name="prefill",
     )(
-        tab,
+        cached_len,
+        new_len,
+        page_table,
+        dest_group,
         queries,
         new_kv,
         cache_now.reshape(2, 16, PAGE, HD),

time: 111 us -> 100 us (0.901)
  the two profiles are of different devices: /device:TPU:40 before, /device:TPU:7 now
where the time goes in v1:
time: 100 us
  Pallas kernels  94.4 us (94%)
  local copies, waits for them, and re-layouts  5.21 us (5%)
    pallas_call x1, Pallas kernels, body(): pl.pallas_call(kernel, out_shape=(jax.ShapeDtypeStruct((64, WIDTH), BF),...  94.4 us
    unnamed x2, local copies, waits for them, and re-layouts  5.21 us

profile of v1, /device:TPU:7, one launch (start us, length us, event | category | flops | bytes accessed | tf_op | source)
XLA Modules:
  0.0 100.3 jit_solution(9153820403446423945)
XLA Ops:
  0.6 94.4 %prefill.1 = (bf16[64,7168]{1,0:T(8,128)(2,1)}, bf16[4,2,8,128,128]{4,3,2,1,0:T(8,128)(2,1)}) custom-call(s32[16]{0:T(128)} %cached_len.1, s32[16]{0:T(128)} %new_len.1, s32[16,16]{1,0:T(8,128)} %pages.1, s32[16]{0:T(128)} %groups.1, bf16[512,896]{1,0:T(8,128)(2,1)} %q_hbm.1, bf16[2,512,128]{2,1,0:T(8,128)(2,1)} %nkv_hbm.1, ...), custom_call_target="tpu_custom_call" | custom-call | tf_op jit(solution)/shard_map/prefill/pallas_call | solution.py:390
  95.1 2.2 %copy.14 = bf16[64,7168]{1,0:T(8,128)(2,1)} copy(bf16[64,7168]{1,0:T(8,128)(2,1)} %get-tuple-element.8) | data formatting | bytes 1835008
  97.2 3.0 %copy.15 = bf16[2,2,2048,128]{3,2,1,0:T(8,128)(2,1)} copy(bf16[2,2,2048,128]{3,2,1,0:T(8,128)(2,1)} %bitcast.4) | data formatting | bytes 4194304

commit v2 on v1

--- a/solution.py
+++ b/solution.py
@@ -30,7 +30,6 @@
 CHUNK = 512
 MASKED = -1e30
 EXP_SCALE = math.log2(math.e) / math.sqrt(HD)
-Z_STEP = (2, 1, 3, 0)
 
 
 def rdma(src, dst, ssem, rsem, dev):
@@ -45,7 +44,7 @@
     q_v, nkv_v, cnow_v, cprev_v, w_v, res_v,
     snow, rnow, sprev, rprev, stage,
     kb, vb, qs, sbuf, att, part,
-    xs, zfar, znear, xr, xfar, xnear, zxs, zxr,
+    xs, zfar, znear, xr, xrn, xfar, xnear, zxs, zxr,
     ld_sem, now_ss, now_rs, prev_ss, prev_rs, core_sem,
     zfar_ss, zfar_rs, znear_ss, znear_rs, xr_ss, xr_rs, xfar_ss, xfar_rs, xnear_ss, xnear_rs,
     zx_ss, zx_rs,
@@ -176,36 +175,54 @@
     loads[4].wait()
     loads[5].wait()
 
-    def zfar_copy(side):
-        half = part.at[0, ZA * side : ZA * (side + 1)]
-        return rdma(half, zfar.at[side], zfar_ss.at[side], zfar_rs.at[side], (up, down)[side])
-
-    def znear_copy(side, g):
-        i = side * NZ + g
+    mine = pl.ds(pl.multiple_of(hi * 64, 64), 64)
+    other = pl.ds(pl.multiple_of((1 - hi) * 64, 64), 64)
+
+    def zfar_copy(side, i):
+        k = side * ZA + i
+        return rdma(part.at[0, k], zfar.at[side, i], zfar_ss.at[k], zfar_rs.at[k], (up, down)[side])
+
+    def znear_copy(side, g, half):
+        i = (side * NZ + g) * 2 + half
         return rdma(
-            part.at[1 + side, g], znear.at[side, g], znear_ss.at[i], znear_rs.at[i], (up, down)[side]
+            part.at[1 + half, g, side * 64 : (side + 1) * 64],
+            znear.at[side, g, half * 64 : (half + 1) * 64],
+            znear_ss.at[i], znear_rs.at[i], (up, down)[side],
         )
 
-    def xr_copy(rel):
-        rows = pl.ds(pl.multiple_of((1 - hi) * 64, 64), 64)
-        return rdma(part.at[rel, NZ:GROUPS, rows], xr.at[rel], xr_ss.at[rel], xr_rs.at[rel], across)
+    def xr_copy(part_of):
+        if part_of == 1:
+            return rdma(part.at[1, NZ:GROUPS], xrn, xr_ss.at[1], xr_rs.at[1], across)
+        src = part.at[3 * part_of // 2, NZ:GROUPS, other]
+        return rdma(src, xr.at[part_of // 2], xr_ss.at[part_of], xr_rs.at[part_of], across)
+
+    def pass_on(half):
+        rows = (other, mine)[half]
+        for i in range(ZA):
+            for side in range(2):
+                g = side * ZA + i
+                cut = slice(side * 64, (side + 1) * 64)
+                part[1 + half, g, cut, :] = (
+                    part[1 + half, g, cut, :].astype(F32) + zfar[side, i, rows, :].astype(F32)
+                ).astype(BF)
+                znear_copy(side, g, half).start()
 
     def block(rel, _):
-        @pl.when(rel == 3)
-        def _():
-            zfar_copy(0).wait_recv()
-            for g in range(ZA):
-                part[1, g] = (part[1, g].astype(F32) + zfar[0, g].astype(F32)).astype(BF)
-                znear_copy(0, g).start()
-            zfar_copy(1).wait_recv()
-            for g in range(ZA):
-                part[2, ZA + g] = (part[2, ZA + g].astype(F32) + zfar[1, g].astype(F32)).astype(BF)
-                znear_copy(1, ZA + g).start()
-
-        zb = (z + jnp.where(rel == 0, 2, jnp.where(rel == 1, 1, jnp.where(rel == 2, 3, 0)))) % 4
-        row = pl.multiple_of(zb * PAGE, PAGE)
+        near = (rel == 1) | (rel == 2)
+        part_row = jnp.where(rel == 1, 1 - hi, hi) * 64
+        above = ((z + 1) % 4) * PAGE + part_row
+        below = ((z + 3) % 4) * PAGE + part_row
+        whole = jnp.where(rel == 0, (z + 2) % 4, z) * PAGE
+        row_a = pl.multiple_of(jnp.where(near, above, whole), 64)
+        row_b = pl.multiple_of(jnp.where(near, below, whole + 64), 64)
         for h in range(HEADS):
-            qs[h * PAGE : (h + 1) * PAGE, :HD] = q_v[pl.ds(row, PAGE), h * HD : (h + 1) * HD]
+            qs[h * PAGE : h * PAGE + 64, :HD] = q_v[pl.ds(row_a, 64), h * HD : (h + 1) * HD]
+            qs[h * PAGE + 64 : (h + 1) * PAGE, :HD] = q_v[pl.ds(row_b, 64), h * HD : (h + 1) * HD]
+
+        def position(shape):
+            r = lax.broadcasted_iota(jnp.int32, shape, 0)
+            return r + jnp.where(r < 64, row_a, row_b - 64)
+
         top = None
         for ch in range(KEYS // CHUNK):
             sc = lax.dot_general(
@@ -213,7 +230,7 @@
                 preferred_element_type=F32,
             )
             if ch == KEYS // CHUNK - 1:
-                qpos = row + lax.broadcasted_iota(jnp.int32, (PAGE, CHUNK), 0)
+                qpos = position((PAGE, CHUNK))
                 kpos = lax.broadcasted_iota(jnp.int32, (PAGE, CHUNK), 1)
                 bias = jnp.where(kpos <= qpos, 0.0, MASKED)
                 sc = (sc.reshape(HEADS, PAGE, CHUNK) + bias[None]).reshape(HEADS * PAGE, CHUNK)
@@ -228,44 +245,68 @@
             prod = jnp.dot(wts, vb[ch * CHUNK : (ch + 1) * CHUNK, :], preferred_element_type=F32)
             acc = prod if acc is None else acc + prod
         out = acc[:, :HD] / acc[:, HD:]
-        live = row + lax.broadcasted_iota(jnp.int32, (PAGE, HD), 0) < fresh_count
+        live = position((PAGE, HD)) < fresh_count
         for h in range(HEADS):
             att[:, h * HD : (h + 1) * HD] = jnp.where(live, out[h * PAGE : (h + 1) * PAGE], 0.0).astype(BF)
 
-        def project(g, _):
+        @pl.when(rel == 2)
+        def _():
+            for side in range(2):
+                for i in range(ZA):
+                    zfar_copy(side, i).wait_recv()
+            pass_on(0)
+
+        def project(g):
             cols = pl.ds(pl.multiple_of(g * GW, GW), GW)
             part[rel, g] = jnp.dot(att[...], w_v[:, cols], preferred_element_type=F32).astype(BF)
+
+        def z_first(i, _):
+            for side in range(2):
+                project(side * ZA + i)
+
+                @pl.when(rel == 0)
+                def _():
+                    zfar_copy(side, i).start()
+
             return 0
 
-        lax.fori_loop(0, GROUPS, project, 0)
-
-        @pl.when(rel == 0)
-        def _():
-            zfar_copy(0).start()
-            zfar_copy(1).start()
-
-        @pl.when(rel == 1)
-        def _():
-            for g in range(ZA, NZ):
-                znear_copy(0, g).start()
+        def x_first(g, _):
+            project(g)
+            return 0
+
+        lax.fori_loop(0, ZA, z_first, 0)
+
+        for half in range(2):
+
+            @pl.when(rel == 1 + half)
+            def _():
+                for i in range(ZA):
+                    znear_copy(0, ZA + i, half).start()
+                    znear_copy(1, i, half).start()
+
+        lax.fori_loop(NZ, GROUPS, x_first, 0)
+        for part_of in range(3):
+
+            @pl.when(rel == (0, 1, 3)[part_of])
+            def _():
+                xr_copy(part_of).start()
 
         @pl.when(rel == 2)
         def _():
-            for g in range(ZA):
-                znear_copy(1, g).start()
-
-        xr_copy(rel).start()
+            pass_on(1)
+
         return 0
 
     lax.fori_loop(0, 4, block, 0)
 
-    mine = pl.ds(pl.multiple_of(hi * 64, 64), 64)
-    other = pl.ds(pl.multiple_of((1 - hi) * 64, 64), 64)
-
     def pair_sum(rel):
-        xr_copy(rel).wait_recv()
         for g in range(NX):
-            xs[rel, g] = (part[rel, NZ + g, mine, :].astype(F32) + xr[rel, g].astype(F32)).astype(BF)
+            if rel == 0:
+                own, got = part[0, NZ + g, mine, :], xr[0, g]
+            else:
+                cut = slice((rel - 1) * 64, rel * 64)
+                own, got = part[2, NZ + g, cut, :], xrn[g, cut]
+            xs[rel, g] = (own.astype(F32) + got.astype(F32)).astype(BF)
 
     def xfar_copy(side):
         half = xs.at[0, XB * side : XB * (side + 1)]
@@ -278,9 +319,11 @@
             xs.at[1 + side, cols], xnear.at[side, cols], xnear_ss.at[i], xnear_rs.at[i], (up, down)[side]
         )
 
+    xr_copy(0).wait_recv()
     pair_sum(0)
     xfar_copy(0).start()
     xfar_copy(1).start()
+    xr_copy(1).wait_recv()
     pair_sum(1)
     xnear_copy(0, 1).start()
     pair_sum(2)
@@ -319,10 +362,10 @@
 
     order = [g for pair in zip(range(ZA), range(ZA, NZ)) for g in pair]
     for g in order:
-        znear_copy(0, g).wait_recv()
-        znear_copy(1, g).wait_recv()
+        znear_copy(0, g, 0).wait_recv()
+        znear_copy(1, g, 0).wait_recv()
         zxs[g] = (
-            part[3, g, other, :].astype(F32) + znear[0, g, other, :].astype(F32) + znear[1, g, other, :].astype(F32)
+            part[3, g, other, :].astype(F32) + znear[0, g, :64].astype(F32) + znear[1, g, :64].astype(F32)
         ).astype(BF)
         zx_copy(g).start()
 
@@ -334,16 +377,18 @@
     for g in range(XB):
         xs[2, XB + g] = (xs[2, XB + g].astype(F32) + xfar[1, g].astype(F32)).astype(BF)
     xnear_copy(1, 1).start()
-    xr_copy(3).wait_recv()
+    xr_copy(2).wait_recv()
 
     for g in order:
         zx_copy(g).wait_recv()
+        znear_copy(0, g, 1).wait_recv()
+        znear_copy(1, g, 1).wait_recv()
         cols = slice(g * GW, (g + 1) * GW)
         mixed_ref[:, cols] = (
             res_v[:, cols].astype(F32)
             + part[3, g, mine, :].astype(F32)
-            + znear[0, g, mine, :].astype(F32)
-            + znear[1, g, mine, :].astype(F32)
+            + znear[0, g, 64:].astype(F32)
+            + znear[1, g, 64:].astype(F32)
             + zxr[g].astype(F32)
         ).astype(BF)
     for side in range(2):
@@ -354,7 +399,7 @@
         mixed_ref[:, cols] = (
             res_v[:, cols].astype(F32)
             + part[3, NZ + g, mine, :].astype(F32)
-            + xr[3, g].astype(F32)
+            + xr[1, g].astype(F32)
             + xnear[0, g].astype(F32)
             + xnear[1, g].astype(F32)
         ).astype(BF)
@@ -367,14 +412,16 @@
 
     lax.fori_loop(1, N_SEQ, drain, 0)
     for side in range(2):
-        zfar_copy(side).wait_send()
+        for i in range(ZA):
+            zfar_copy(side, i).wait_send()
         xfar_copy(side).wait_send()
         for g in range(NZ):
-            znear_copy(side, g).wait_send()
+            znear_copy(side, g, 0).wait_send()
+            znear_copy(side, g, 1).wait_send()
         for half in range(2):
             xnear_copy(side, half).wait_send()
-    for rel in range(4):
-        xr_copy(rel).wait_send()
+    for part_of in range(3):
+        xr_copy(part_of).wait_send()
     for g in range(NZ):
         zx_copy(g).wait_send()
     core_copy.wait_send()
@@ -416,14 +463,15 @@
             vm((3, NX, 64, GW), BF),
             vm((2, ZA, PAGE, GW), BF),
             vm((2, NZ, PAGE, GW), BF),
-            vm((4, NX, 64, GW), BF),
+            vm((2, NX, 64, GW), BF),
+            vm((NX, PAGE, GW), BF),
             vm((2, XB, 64, GW), BF),
             vm((2, NX, 64, GW), BF),
             vm((NZ, 64, GW), BF),
             vm((NZ, 64, GW), BF),
             dma((6,)),
             dma((16,)), dma((16,)), dma((16,)), dma((16,)), dma((2,)),
-            dma((2,)), dma((2,)), dma((2 * NZ,)), dma((2 * NZ,)), dma((4,)), dma((4,)),
+            dma((NZ,)), dma((NZ,)), dma((4 * NZ,)), dma((4 * NZ,)), dma((3,)), dma((3,)),
             dma((2,)), dma((2,)), dma((4,)), dma((4,)), dma((NZ,)), dma((NZ,)),
         ],
         compiler_params=pltpu.CompilerParams(

time: 100 us -> 97.3 us (0.973)
  the two profiles are of different devices: /device:TPU:7 before, /device:TPU:40 now
where the time goes in v2:
time: 97.3 us; the launch traced here: 97 us
  Pallas kernels  91.2 us (94%)
  local copies, waits for them, and re-layouts  5.21 us (5%)
    pallas_call x1, Pallas kernels, body(): pl.pallas_call(kernel, out_shape=(jax.ShapeDtypeStruct((64, WIDTH), BF),...  91.2 us
    unnamed x2, local copies, waits for them, and re-layouts  5.21 us

profile of v2, /device:TPU:40, one launch (start us, length us, event | category | flops | bytes accessed | tf_op | source)
XLA Modules:
  0.0 97.0 jit_solution(543674066128342255)
XLA Ops:
  0.6 91.2 %prefill.1 = (bf16[64,7168]{1,0:T(8,128)(2,1)}, bf16[4,2,8,128,128]{4,3,2,1,0:T(8,128)(2,1)}) custom-call(s32[16]{0:T(128)} %cached_len.1, s32[16]{0:T(128)} %new_len.1, s32[16,16]{1,0:T(8,128)} %pages.1, s32[16]{0:T(128)} %groups.1, bf16[512,896]{1,0:T(8,128)(2,1)} %q_hbm.1, bf16[2,512,128]{2,1,0:T(8,128)(2,1)} %nkv_hbm.1, ...), custom_call_target="tpu_custom_call" | custom-call | tf_op jit(solution)/shard_map/prefill/pallas_call | solution.py:437
  91.8 2.2 %copy.14 = bf16[64,7168]{1,0:T(8,128)(2,1)} copy(bf16[64,7168]{1,0:T(8,128)(2,1)} %get-tuple-element.8) | data formatting | bytes 1835008
  94.0 3.0 %copy.15 = bf16[2,2,2048,128]{3,2,1,0:T(8,128)(2,1)} copy(bf16[2,2,2048,128]{3,2,1,0:T(8,128)(2,1)} %bitcast.4) | data formatting | bytes 4194304
